TPU v7x, 256 devices: a whole 4x4x8 slice. The times are simulated.
256 devices in a mesh: px: 4 (over y_lo, core), py: 8 (over x, y_hi), dom: 8 (over z).
Axes of the slice: x: 4, y: 4 (y_hi: 2, y_lo: 2; y = y_hi * 2 + y_lo), z: 8, core: 2. Of those that a mesh axis runs over, the one named last changes fastest.
Arguments:
- velocity: float32 [16, 64, 256, 128], P('dom', 'px', 'py'), may hold values from 0.65 to 2.2
- buoyancy: float32 [64, 256, 128], P('px', 'py'), may hold values from 0.6 to 1.6
- forward_prev: float32 [16, 64, 256, 128], P('dom', 'px', 'py'), may hold values from -12 to 12
- forward_now: float32 [16, 64, 256, 128], P('dom', 'px', 'py'), may hold values from -12 to 12
- adjoint_prev: float32 [16, 64, 256, 128], P('dom', 'px', 'py'), may hold values from -12 to 12
- adjoint_now: float32 [16, 64, 256, 128], P('dom', 'px', 'py'), may hold values from -12 to 12
- sources: int32 [16], P('dom'), may hold values from 0 to 2097151
- wavelet: float32 [16, 3], P('dom'), may hold values from -800 to 800
- receivers: int32 [16, 1024], P('dom'), may hold values from 0 to 2097151
- misfit: float32 [16, 3, 1024], P('dom'), may hold values from -6 to 6
- sponge: int32 [6], replicated, may hold values from 2 to 8
Outputs:
- forward_before: float32 [16, 64, 256, 128], P('dom', 'px', 'py')
- forward_after: float32 [16, 64, 256, 128], P('dom', 'px', 'py')
- adjoint_before: float32 [16, 64, 256, 128], P('dom', 'px', 'py')
- adjoint_after: float32 [16, 64, 256, 128], P('dom', 'px', 'py')
- drift: float32 [16, 64, 256, 128], P('dom', 'px', 'py')
- spread: float32 [16, 64, 256, 128], P('dom', 'px', 'py')
All inputs are finite; a program needn't handle non-finite values.
Results may differ from a plain program's by a relative error of at most 0.0003.
Values sent between devices are 32-bit elements; how exact they have to be, the bound alone decides.
A program may use at most 64 MiB of HBM per device.

v0:
```python
import jax
import jax.numpy as jnp
from jax import lax
from jax.sharding import PartitionSpec as P

EPSILON = 1e-06
TIME_STEP = 0.18
SPONGE_RATE = 0.5
NEAR_WEIGHT = 9.0 / 8.0
FAR_WEIGHT = 1.0 / 24.0


def with_halo(cells, sides, width):
    for axis, dim in sides:
        count = lax.axis_size(axis)
        ends = count - 1
        head = lax.slice_in_dim(cells, 0, width, axis=dim)
        tail = lax.slice_in_dim(cells, cells.shape[dim] - width, cells.shape[dim], axis=dim)
        cells = jnp.concatenate(
            [
                lax.ppermute(tail, axis, [(i, (i + 1) % count) for i in range(ends)]),
                cells,
                lax.ppermute(head, axis, [((i + 1) % count, i) for i in range(ends)]),
            ],
            axis=dim,
        )
    return cells


def take_slab(source_array, start_at, amount, which_axis):
    return lax.slice_in_dim(
        source_array, start_at, start_at + amount, axis=source_array.ndim + which_axis
    )


def axis_term(wave_field, buoy_field, extent, which_axis):
    half_buoy = 0.5 * (
        take_slab(buoy_field, 1, extent + 3, which_axis)
        + take_slab(buoy_field, 2, extent + 3, which_axis)
    )
    slope_face = NEAR_WEIGHT * (
        take_slab(wave_field, 2, extent + 3, which_axis)
        - take_slab(wave_field, 1, extent + 3, which_axis)
    ) - FAR_WEIGHT * (
        take_slab(wave_field, 3, extent + 3, which_axis)
        - take_slab(wave_field, 0, extent + 3, which_axis)
    )
    flux_face = half_buoy * slope_face
    return NEAR_WEIGHT * (
        take_slab(flux_face, 2, extent, which_axis) - take_slab(flux_face, 1, extent, which_axis)
    ) - FAR_WEIGHT * (
        take_slab(flux_face, 3, extent, which_axis) - take_slab(flux_face, 0, extent, which_axis)
    )


def divergence(padded, buoy_pad):
    size_x = padded.shape[-3] - 6
    size_y = padded.shape[-2] - 6
    size_z = padded.shape[-1] - 6
    along_x = axis_term(
        padded[..., 3 : size_y + 3, 3 : size_z + 3],
        buoy_pad[:, 3 : size_y + 3, 3 : size_z + 3],
        size_x,
        -3,
    )
    along_y = axis_term(
        padded[..., 3 : size_x + 3, :, 3 : size_z + 3],
        buoy_pad[3 : size_x + 3, :, 3 : size_z + 3],
        size_y,
        -2,
    )
    along_z = axis_term(
        padded[..., 3 : size_x + 3, 3 : size_y + 3, :],
        buoy_pad[3 : size_x + 3, 3 : size_y + 3, :],
        size_z,
        -1,
    )
    return along_x + along_y + along_z


def sponge_term(coords, length, low_width, high_width):
    position = coords.astype(jnp.float32)
    far_side = length - 1 - position
    low_float = low_width.astype(jnp.float32)
    high_float = high_width.astype(jnp.float32)
    low_part = jnp.where(
        position < low_float, jnp.square(SPONGE_RATE * (low_float - position) / low_float), 0.0
    )
    high_part = jnp.where(
        far_side < high_float, jnp.square(SPONGE_RATE * (high_float - far_side) / high_float), 0.0
    )
    return low_part + high_part


def plane_tables(flat_index, size_x, size_y, size_z, total_y):
    plane_size = total_y * size_z
    global_x = flat_index // plane_size
    global_y = flat_index // size_z % total_y
    global_z = flat_index % size_z
    local_x = global_x - lax.axis_index("px") * size_x
    local_y = global_y - lax.axis_index("py") * size_y
    inside = (local_x >= 0) & (local_x < size_x) & (local_y >= 0) & (local_y < size_y)
    plane_at = jnp.where(inside, local_x * size_y + local_y, -1)
    plane_hot = (plane_at[..., None] == lax.iota(jnp.int32, size_x * size_y)).astype(jnp.float32)
    depth_hot = (global_z[..., None] == lax.iota(jnp.int32, size_z)).astype(jnp.float32)
    return (plane_hot, depth_hot)


def kernel_from(gram_total, particles):
    diag_part = jnp.diagonal(gram_total)
    dist_sq = diag_part[:, None] + diag_part[None, :] - 2.0 * gram_total
    width = jnp.sum(dist_sq) / (particles * (particles - 1)) + EPSILON
    kernel = jnp.exp(-dist_sq / width)
    return (kernel, jnp.sum(kernel, axis=1))


def on_device(
    velocity,
    buoyancy,
    forward_prev,
    forward_now,
    adjoint_prev,
    adjoint_now,
    sources,
    wavelet,
    receivers,
    misfit,
    sponge,
):
    part_dev, size_x, size_y, size_z = velocity.shape
    block_cells = size_x * size_y * size_z
    total_x = size_x * lax.axis_size("px")
    total_y = size_y * lax.axis_size("py")
    total_cells = total_x * total_y * size_z
    particles = part_dev * lax.axis_size("dom")
    step_sq = TIME_STEP * TIME_STEP
    coords_x = lax.iota(jnp.int32, size_x) + lax.axis_index("px") * size_x
    coords_y = lax.iota(jnp.int32, size_y) + lax.axis_index("py") * size_y
    coords_z = lax.iota(jnp.int32, size_z)
    damping = jnp.exp(
        -(
            sponge_term(coords_x, total_x, sponge[0], sponge[1])[:, None, None]
            + sponge_term(coords_y, total_y, sponge[2], sponge[3])[None, :, None]
            + sponge_term(coords_z, size_z, sponge[4], sponge[5])[None, None, :]
        )
    )
    buoy_rim = with_halo(buoyancy, (("px", 0), ("py", 1)), 3)
    buoy_pad = jnp.pad(buoy_rim, ((0, 0), (0, 0), (3, 3)))
    wave_scale = velocity * velocity / buoyancy
    grad_coef = -2.0 / (velocity * velocity * velocity)
    src_plane, src_depth = plane_tables(sources, size_x, size_y, size_z, total_y)
    src_pattern = (src_plane[:, :, None] * src_depth[:, None, :]).reshape(velocity.shape)
    rec_plane, rec_depth = plane_tables(receivers, size_x, size_y, size_z, total_y)
    previous = jnp.stack([forward_prev, adjoint_prev])
    current = jnp.stack([forward_now, adjoint_now])
    gradient = jnp.zeros_like(velocity)
    for step_at in range(wavelet.shape[1]):
        rimmed = with_halo(current, (("px", 2), ("py", 3)), 3)
        padded = jnp.pad(rimmed, ((0, 0), (0, 0), (0, 0), (0, 0), (3, 3)))
        stepped = 2.0 * current - previous + step_sq * (wave_scale * divergence(padded, buoy_pad))
        weighted_depth = rec_depth * (step_sq * misfit[:, step_at, :])[:, :, None]
        rec_field = jnp.einsum(
            "prq,prz->pqz",
            rec_plane,
            weighted_depth,
            precision=lax.Precision.HIGHEST,
            preferred_element_type=jnp.float32,
        )
        src_field = src_pattern * (step_sq * wavelet[:, step_at])[:, None, None, None]
        injected = jnp.stack(
            [stepped[0] + src_field, stepped[1] + rec_field.reshape(velocity.shape)]
        )
        advanced = damping * injected
        gradient = gradient + grad_coef * current[1] * (
            advanced[0] - 2.0 * current[0] + previous[0]
        )
        previous, current = (current, advanced)
    flat_model = velocity.reshape(part_dev, block_cells)
    flat_grad = gradient.reshape(part_dev, block_cells)
    dom_start = lax.axis_index("dom") * part_dev
    own_sq = lax.psum(jnp.sum(flat_grad * flat_grad, axis=1), ("px", "py"))
    flat_grad = flat_grad / jnp.sqrt(own_sq / total_cells + EPSILON)[:, None]
    model_cols, grad_cols = (
        lax.all_to_all(flat_model, "dom", split_axis=1, concat_axis=0, tiled=True),
        lax.all_to_all(flat_grad, "dom", split_axis=1, concat_axis=0, tiled=True),
    )
    centered = model_cols - jnp.mean(model_cols, axis=0, keepdims=True)
    gram_part = jnp.dot(
        centered, centered.T, precision=lax.Precision.HIGHEST, preferred_element_type=jnp.float32
    )
    gram_total = lax.psum(gram_part, ("px", "py", "dom"))
    kernel, row_sum = kernel_from(gram_total, particles)
    mixed_grad = jnp.dot(
        kernel, grad_cols, precision=lax.Precision.HIGHEST, preferred_element_type=jnp.float32
    )
    mixed_model = jnp.dot(
        kernel, model_cols, precision=lax.Precision.HIGHEST, preferred_element_type=jnp.float32
    )
    drift_flat, model_mix = (
        lax.all_to_all(mixed_grad, "dom", split_axis=0, concat_axis=1, tiled=True),
        lax.all_to_all(mixed_model, "dom", split_axis=0, concat_axis=1, tiled=True),
    )
    own_rowsum = lax.dynamic_slice_in_dim(row_sum, dom_start, part_dev)
    spread_flat = flat_model * own_rowsum[:, None] - model_mix
    return (
        previous[0],
        current[0],
        previous[1],
        current[1],
        drift_flat.reshape(velocity.shape),
        spread_flat.reshape(velocity.shape),
    )


def solution(mesh):
    placed = (
        P("dom", "px", "py", None),
        P("px", "py", None),
        P("dom", "px", "py", None),
        P("dom", "px", "py", None),
        P("dom", "px", "py", None),
        P("dom", "px", "py", None),
        P("dom"),
        P("dom", None),
        P("dom", None),
        P("dom", None, None),
        P(),
    )
    return jax.shard_map(
        on_device,
        mesh=mesh,
        in_specs=placed,
        out_specs=(
            P("dom", "px", "py", None),
            P("dom", "px", "py", None),
            P("dom", "px", "py", None),
            P("dom", "px", "py", None),
            P("dom", "px", "py", None),
            P("dom", "px", "py", None),
        ),
        check_vma=False,
    )
```

profile of v0, /device:TPU:1, one launch (start us, length us, event | category | flops | bytes accessed | tf_op | source)
XLA Modules:
  0.0 337.7 jit_solution(8753166672885361764)
XLA Ops:
  2.5 5.1 %collective-permute-start.3 = (f32[2,2,3,32,128]{4,3,2,1,0:T(8,128)}, f32[2,2,3,32,128]{4,3,2,1,0:T(8,128)S(1)}, u32[]{:S(2)}, u32[]{:S(2)}) collective-permute-start(f32[2,2,3,32,128]{4,3,2,1,0:T(8,128)} %get-tuple-element.33), channel_id=1, source_target_pairs={{64,0},{128,64},{192,128},{65,1},{129,65},{193,129},{66,2},{130,66... | collective-permute-start | bytes 589832 | tf_op jit(solution)/shard_map/ppermute | solution.py:23
  7.6 1.9 collective-permute-start.2
  9.5 1.9 collective-permute-start
  11.5 2.4 collective-permute-start.1
  15.3 7.7 %all-to-all-start = ((f32[2,8,8192]{2,0,1:T(2,128)}), f32[2,8,8192]{2,0,1:T(2,128)S(1)}, u32[]{:S(2)}, u32[]{:S(2)}) async-start(f32[2,8,8192]{2,0,1:T(2,128)} %copy.54), calls=%async_computation | async-start | bytes 1048576 | tf_op jit(solution)/shard_map/all_to_all | solution.py:184
  28.1 3.2 fusion.2
  32.7 5.5 %collective-permute-start.4 = (f32[22,3,128]{2,1,0:T(4,128)S(1)}, f32[22,3,128]{2,1,0:T(4,128)S(1)}, u32[]{:S(2)}, u32[]{:S(2)}) collective-permute-start(f32[22,3,128]{2,1,0:T(4,128)S(1)} %get-tuple-element.36), channel_id=1, source_target_pairs={{0,8},{8,16},{16,24},{24,32},{32,40},{40,48},{48,56},{1,9},{9,17},... | collective-permute-start | bytes 101384 | tf_op jit(solution)/shard_map/ppermute | solution.py:21
  42.3 6.9 %collective-permute-start.6 = (f32[2,2,22,3,128]{4,3,2,1,0:T(4,128)}, f32[2,2,22,3,128]{4,3,2,1,0:T(4,128)}, u32[]{:S(2)}, u32[]{:S(2)}) collective-permute-start(f32[2,2,22,3,128]{4,3,2,1,0:T(4,128)} %get-tuple-element.20), channel_id=1, source_target_pairs={{0,8},{8,16},{16,24},{24,32},{32,40},{40,48},{48,56},{1,9},{9,17},... | collective-permute-start | bytes 405512 | tf_op jit(solution)/shard_map/ppermute | solution.py:21
  54.3 79.6 %psum.14 = f32[16,16]{1,0:T(8,128)S(1)} all-reduce(f32[16,16]{1,0:T(8,128)S(1)} %fusion.141), channel_id=1, replica_groups=mesh['px'=4,'py'=8,'dom'=8] {'px','py','dom'}, use_global_device_ids=true, to_apply=%region_1.2 | all-reduce | flops 256 | bytes 2048 | tf_op jit(solution)/shard_map/psum | solution.py:191
  137.9 5.5 %all-to-all-start.3 = ((f32[8,2,8192]{2,1,0:T(2,128)}), f32[8,2,8192]{2,1,0:T(2,128)}, u32[]{:S(2)}, u32[]{:S(2)}) async-start(f32[8,2,8192]{2,1,0:T(2,128)} %copy.60), calls=%async_computation.3 | async-start | bytes 1048576 | tf_op jit(solution)/shard_map/all_to_all | solution.py:201
  143.3 2.4 fusion.47
  147.1 3.1 fusion.6
  150.2 2.6 fusion.37
  152.8 8.6 %all-to-all-done.3 = f32[8,2,8192]{2,1,0:T(2,128)} async-done(((f32[8,2,8192]{2,1,0:T(2,128)}), f32[8,2,8192]{2,1,0:T(2,128)}, u32[]{:S(2)}, u32[]{:S(2)}) %all-to-all-start.3) | async-done | bytes 524320 | tf_op jit(solution)/shard_map/all_to_all | solution.py:201
  161.4 2.1 copy.61
  163.5 1.9 all_to_all.59
  165.5 2.4 multiply_subtract_fusion
  167.8 4.3 %fusion.84 = f32[2,2,16,32,128]{4,3,2,1,0:T(8,128)S(1)} fusion(f32[2,2,16,32,131]{4,3,2,1,0:T(8,128)} %fusion.6, f32[2,2,16,35,128]{4,3,2,1,0:T(8,128)S(1)} %copy-done.2, f32[2,2,19,32,128]{4,3,2,1,0:T(8,128)S(1)} %fusion.47, f32[1,2,16,32,128]{4,3,2,1,0:T(8,128)S(1)} %bitcast.82, f32[1,2,16,32,128]{4,3,2,1,0:T(8,128)S(1)} %bitcast.81, ...), kind=kLoop, calls=%fused_computation.153 | loop fusion | flops 6291456 | bytes 16252928 | tf_op jit(solution)/shard_map/add | solution.py:160
  172.6 2.4 collective-permute-start.9
  175.0 3.2 collective-permute-start.8
  178.2 2.5 fusion.1
  182.1 5.6 %collective-permute-start.10 = (f32[2,2,22,3,128]{4,3,2,1,0:T(4,128)S(1)}, f32[2,2,22,3,128]{4,3,2,1,0:T(4,128)S(1)}, u32[]{:S(2)}, u32[]{:S(2)}) collective-permute-start(f32[2,2,22,3,128]{4,3,2,1,0:T(4,128)S(1)} %get-tuple-element.18), channel_id=1, source_target_pairs={{0,8},{8,16},{16,24},{24,32},{32,40},{40,48},{48,56},{1,9},{9,17},... | collective-permute-start | bytes 405512 | tf_op jit(solution)/shard_map/ppermute | solution.py:21
  190.2 2.4 collective-permute-done.10
  196.9 2.3 collective-permute-start.13
  199.2 3.5 %collective-permute-start.12 = (f32[2,2,3,32,128]{4,3,2,1,0:T(8,128)S(1)}, f32[2,2,3,32,128]{4,3,2,1,0:T(8,128)S(1)}, u32[]{:S(2)}, u32[]{:S(2)}) collective-permute-start(f32[2,2,3,32,128]{4,3,2,1,0:T(8,128)S(1)} %get-tuple-element.24), channel_id=1, source_target_pairs={{0,64},{64,128},{128,192},{1,65},{65,129},{129,193},{2,66},{66,130... | collective-permute-start | bytes 589832 | tf_op jit(solution)/shard_map/ppermute | solution.py:21
  202.7 2.5 fusion
  206.6 6.3 %collective-permute-start.14 = (f32[2,2,22,3,128]{4,3,2,1,0:T(4,128)S(1)}, f32[2,2,22,3,128]{4,3,2,1,0:T(4,128)S(1)}, u32[]{:S(2)}, u32[]{:S(2)}) collective-permute-start(f32[2,2,22,3,128]{4,3,2,1,0:T(4,128)S(1)} %get-tuple-element.16), channel_id=1, source_target_pairs={{0,8},{8,16},{16,24},{24,32},{32,40},{40,48},{48,56},{1,9},{9,17},... | collective-permute-start | bytes 405512 | tf_op jit(solution)/shard_map/ppermute | solution.py:21
  215.1 4.6 %collective-permute-done.14 = f32[2,2,22,3,128]{4,3,2,1,0:T(4,128)S(1)} collective-permute-done((f32[2,2,22,3,128]{4,3,2,1,0:T(4,128)S(1)}, f32[2,2,22,3,128]{4,3,2,1,0:T(4,128)S(1)}, u32[]{:S(2)}, u32[]{:S(2)}) %collective-permute-start.14) | collective-permute-done | bytes 135200 | tf_op jit(solution)/shard_map/ppermute | solution.py:21
  226.5 68.9 %psum.15 = f32[2]{0:T(128)S(1)} all-reduce(f32[2]{0:T(128)S(1)} %get-tuple-element.11), channel_id=1, replica_groups=mesh['px'=4,'py'=8,'dom'=8] {'px','py'}, use_global_device_ids=true, to_apply=%region_4.5 | all-reduce | flops 2 | bytes 16 | tf_op jit(solution)/shard_map/psum | solution.py:181
  295.9 19.1 %all_to_all.64 = f32[2,8,8192]{2,0,1:T(2,128)S(1)} all-to-all(f32[2,8,8192]{2,0,1:T(2,128)S(1)} %copy.55), channel_id=1, replica_groups=mesh['px'=4,'py'=8,'dom'=8] {'dom'}, dimensions={1} | all-to-all | bytes 1048576 | tf_op jit(solution)/shard_map/all_to_all | solution.py:185
  317.1 3.5 %all-to-all-start.2 = ((f32[8,2,8192]{2,1,0:T(2,128)}), f32[8,2,8192]{2,1,0:T(2,128)S(1)}, u32[]{:S(2)}, u32[]{:S(2)}) async-start(f32[8,2,8192]{2,1,0:T(2,128)} %copy.57), calls=%async_computation.2 | async-start | bytes 1048576 | tf_op jit(solution)/shard_map/all_to_all | solution.py:200
  321.5 15.1 %all-to-all-done.2 = f32[8,2,8192]{2,1,0:T(2,128)S(1)} async-done(((f32[8,2,8192]{2,1,0:T(2,128)}), f32[8,2,8192]{2,1,0:T(2,128)S(1)}, u32[]{:S(2)}, u32[]{:S(2)}) %all-to-all-start.2) | async-done | bytes 524320 | tf_op jit(solution)/shard_map/all_to_all | solution.py:200
  (131 shorter events, 43.0 us)
Async XLA Ops:
  0.6 8.9 %copy-start.11 = (f32[16,32,128]{2,1,0:T(8,128)S(1)}, f32[16,32,128]{2,1,0:T(8,128)}, u32[]{:S(2)}) copy-start(f32[16,32,128]{2,1,0:T(8,128)} %param.12) | copy-start | bytes 786436
  0.6 13.2 %copy-start.8 = (f32[2,16,32,128]{3,2,1,0:T(8,128)S(1)}, f32[2,16,32,128]{3,2,1,0:T(8,128)}, u32[]{:S(2)}) copy-start(f32[2,16,32,128]{3,2,1,0:T(8,128)} %param.11) | copy-start | bytes 1572868
  2.5 37.4 %collective-permute-start.3 = (f32[2,2,3,32,128]{4,3,2,1,0:T(8,128)}, f32[2,2,3,32,128]{4,3,2,1,0:T(8,128)S(1)}, u32[]{:S(2)}, u32[]{:S(2)}) collective-permute-start(f32[2,2,3,32,128]{4,3,2,1,0:T(8,128)} %get-tuple-element.33), channel_id=1, source_target_pairs={{64,0},{128,64},{192,128},{65,1},{129,65},{193,129},{66,2},{130,66... | collective-permute-start | bytes 589832 | tf_op jit(solution)/shard_map/ppermute | solution.py:23
  7.6 32.3 %collective-permute-start.2 = (f32[2,2,3,32,128]{4,3,2,1,0:T(8,128)S(1)}, f32[2,2,3,32,128]{4,3,2,1,0:T(8,128)S(1)}, u32[]{:S(2)}, u32[]{:S(2)}) collective-permute-start(f32[2,2,3,32,128]{4,3,2,1,0:T(8,128)S(1)} %get-tuple-element.32), channel_id=1, source_target_pairs={{0,64},{64,128},{128,192},{1,65},{65,129},{129,193},{2,66},{66,130... | collective-permute-start | bytes 589832 | tf_op jit(solution)/shard_map/ppermute | solution.py:21
  9.5 21.8 %collective-permute-start = (f32[3,32,128]{2,1,0:T(8,128)S(1)}, f32[3,32,128]{2,1,0:T(8,128)S(1)}, u32[]{:S(2)}, u32[]{:S(2)}) collective-permute-start(f32[3,32,128]{2,1,0:T(8,128)S(1)} %get-tuple-element.39), channel_id=1, source_target_pairs={{0,64},{64,128},{128,192},{1,65},{65,129},{129,193},{2,66},{66,130... | collective-permute-start | bytes 147464 | tf_op jit(solution)/shard_map/ppermute | solution.py:21
  11.5 19.9 %collective-permute-start.1 = (f32[3,32,128]{2,1,0:T(8,128)S(1)}, f32[3,32,128]{2,1,0:T(8,128)S(1)}, u32[]{:S(2)}, u32[]{:S(2)}) collective-permute-start(f32[3,32,128]{2,1,0:T(8,128)S(1)} %get-tuple-element.38), channel_id=1, source_target_pairs={{64,0},{128,64},{192,128},{65,1},{129,65},{193,129},{66,2},{130,66... | collective-permute-start | bytes 147464 | tf_op jit(solution)/shard_map/ppermute | solution.py:23
  14.0 8.9 %copy-start.16 = (f32[2,3]{1,0:T(2,128)S(1)}, f32[2,3]{1,0:T(2,128)}, u32[]{:S(2)}) copy-start(f32[2,3]{1,0:T(2,128)} %param.18) | copy-start | bytes 76
  14.0 9.2 %copy-start.18 = (s32[2]{0:T(128)S(1)}, s32[2]{0:T(128)}, u32[]{:S(2)}) copy-start(s32[2]{0:T(128)} %param.17) | copy-start | bytes 28
  14.0 9.3 %copy-start.17 = (s32[2,1024]{1,0:T(2,128)S(1)}, s32[2,1024]{1,0:T(2,128)}, u32[]{:S(2)}) copy-start(s32[2,1024]{1,0:T(2,128)} %param.19) | copy-start | bytes 24580
  14.0 9.3 %copy-start.14 = (f32[2,3,1024]{2,0,1:T(2,128)S(1)}, f32[2,3,1024]{2,0,1:T(2,128)}, u32[]{:S(2)}) copy-start(f32[2,3,1024]{2,0,1:T(2,128)} %param.20) | copy-start | bytes 73732
  14.0 9.3 %copy-start.15 = (s32[6]{0:T(128)S(1)}, s32[6]{0:T(128)}, u32[]{:S(2)}) copy-start(s32[6]{0:T(128)} %param.21) | copy-start | bytes 76
  15.3 35.2 %all-to-all-start = ((f32[2,8,8192]{2,0,1:T(2,128)}), f32[2,8,8192]{2,0,1:T(2,128)S(1)}, u32[]{:S(2)}, u32[]{:S(2)}) async-start(f32[2,8,8192]{2,0,1:T(2,128)} %copy.54), calls=%async_computation | async-start | bytes 1048576 | tf_op jit(solution)/shard_map/all_to_all | solution.py:184
  31.4 7.6 %collective-permute-start.5 = (f32[22,3,128]{2,1,0:T(4,128)S(1)}, f32[22,3,128]{2,1,0:T(4,128)S(1)}, u32[]{:S(2)}, u32[]{:S(2)}) collective-permute-start(f32[22,3,128]{2,1,0:T(4,128)S(1)} %get-tuple-element.37), channel_id=1, source_target_pairs={{8,0},{16,8},{24,16},{32,24},{40,32},{48,40},{56,48},{9,1},{17,9},... | collective-permute-start | bytes 101384 | tf_op jit(solution)/shard_map/ppermute | solution.py:23
  32.7 6.6 %collective-permute-start.4 = (f32[22,3,128]{2,1,0:T(4,128)S(1)}, f32[22,3,128]{2,1,0:T(4,128)S(1)}, u32[]{:S(2)}, u32[]{:S(2)}) collective-permute-start(f32[22,3,128]{2,1,0:T(4,128)S(1)} %get-tuple-element.36), channel_id=1, source_target_pairs={{0,8},{8,16},{16,24},{24,32},{32,40},{40,48},{48,56},{1,9},{9,17},... | collective-permute-start | bytes 101384 | tf_op jit(solution)/shard_map/ppermute | solution.py:21
  39.9 10.6 %copy-start.4 = (f32[2,2,3,32,128]{4,3,2,1,0:T(8,128)}, f32[2,2,3,32,128]{4,3,2,1,0:T(8,128)S(1)}, u32[]{:S(2)}) copy-start(f32[2,2,3,32,128]{4,3,2,1,0:T(8,128)S(1)} %collective-permute-done.3) | copy-start | bytes 589828
  40.2 10.3 %copy-start.6 = (f32[2,2,3,32,128]{4,3,2,1,0:T(8,128)}, f32[2,2,3,32,128]{4,3,2,1,0:T(8,128)S(1)}, u32[]{:S(2)}) copy-start(f32[2,2,3,32,128]{4,3,2,1,0:T(8,128)S(1)} %collective-permute-done.2) | copy-start | bytes 589828
  41.0 104.7 %collective-permute-start.7 = (f32[2,2,22,3,128]{4,3,2,1,0:T(4,128)}, f32[2,2,22,3,128]{4,3,2,1,0:T(4,128)}, u32[]{:S(2)}, u32[]{:S(2)}) collective-permute-start(f32[2,2,22,3,128]{4,3,2,1,0:T(4,128)} %get-tuple-element.21), channel_id=1, source_target_pairs={{8,0},{16,8},{24,16},{32,24},{40,32},{48,40},{56,48},{9,1},{17,9},... | collective-permute-start | bytes 405512 | tf_op jit(solution)/shard_map/ppermute | solution.py:23
  42.3 103.5 %collective-permute-start.6 = (f32[2,2,22,3,128]{4,3,2,1,0:T(4,128)}, f32[2,2,22,3,128]{4,3,2,1,0:T(4,128)}, u32[]{:S(2)}, u32[]{:S(2)}) collective-permute-start(f32[2,2,22,3,128]{4,3,2,1,0:T(4,128)} %get-tuple-element.20), channel_id=1, source_target_pairs={{0,8},{8,16},{16,24},{24,32},{32,40},{40,48},{48,56},{1,9},{9,17},... | collective-permute-start | bytes 405512 | tf_op jit(solution)/shard_map/ppermute | solution.py:21
  137.9 23.5 %all-to-all-start.3 = ((f32[8,2,8192]{2,1,0:T(2,128)}), f32[8,2,8192]{2,1,0:T(2,128)}, u32[]{:S(2)}, u32[]{:S(2)}) async-start(f32[8,2,8192]{2,1,0:T(2,128)} %copy.60), calls=%async_computation.3 | async-start | bytes 1048576 | tf_op jit(solution)/shard_map/all_to_all | solution.py:201
  143.3 2.5 copy-start.5
  143.3 2.5 copy-start.7
  167.8 4.3 %copy-start.13 = (f32[2,512,128]{2,1,0:T(8,128)S(1)}, f32[2,512,128]{2,1,0:T(8,128)}, u32[]{:S(2)}) copy-start(f32[2,512,128]{2,1,0:T(8,128)} %fusion.2) | copy-start | bytes 1572868
  172.6 8.1 %collective-permute-start.9 = (f32[2,2,3,32,128]{4,3,2,1,0:T(8,128)S(1)}, f32[2,2,3,32,128]{4,3,2,1,0:T(8,128)S(1)}, u32[]{:S(2)}, u32[]{:S(2)}) collective-permute-start(f32[2,2,3,32,128]{4,3,2,1,0:T(8,128)S(1)} %get-tuple-element.29), channel_id=1, source_target_pairs={{64,0},{128,64},{192,128},{65,1},{129,65},{193,129},{66,2},{130,66... | collective-permute-start | bytes 589832 | tf_op jit(solution)/shard_map/ppermute | solution.py:23
  175.0 5.8 %collective-permute-start.8 = (f32[2,2,3,32,128]{4,3,2,1,0:T(8,128)S(1)}, f32[2,2,3,32,128]{4,3,2,1,0:T(8,128)S(1)}, u32[]{:S(2)}, u32[]{:S(2)}) collective-permute-start(f32[2,2,3,32,128]{4,3,2,1,0:T(8,128)S(1)} %get-tuple-element.28), channel_id=1, source_target_pairs={{0,64},{64,128},{128,192},{1,65},{65,129},{129,193},{2,66},{66,130... | collective-permute-start | bytes 589832 | tf_op jit(solution)/shard_map/ppermute | solution.py:21
  180.8 9.3 %collective-permute-start.11 = (f32[2,2,22,3,128]{4,3,2,1,0:T(4,128)S(1)}, f32[2,2,22,3,128]{4,3,2,1,0:T(4,128)S(1)}, u32[]{:S(2)}, u32[]{:S(2)}) collective-permute-start(f32[2,2,22,3,128]{4,3,2,1,0:T(4,128)S(1)} %get-tuple-element.19), channel_id=1, source_target_pairs={{8,0},{16,8},{24,16},{32,24},{40,32},{48,40},{56,48},{9,1},{17,9},... | collective-permute-start | bytes 405512 | tf_op jit(solution)/shard_map/ppermute | solution.py:23
  182.1 5.8 %copy-start.3 = (f32[19,32,128]{2,1,0:T(8,128)S(1)}, f32[19,32,128]{2,1,0:T(8,128)}, u32[]{:S(2)}) copy-start(f32[19,32,128]{2,1,0:T(8,128)} %fusion.116) | copy-start | bytes 933892
  182.1 10.5 %collective-permute-start.10 = (f32[2,2,22,3,128]{4,3,2,1,0:T(4,128)S(1)}, f32[2,2,22,3,128]{4,3,2,1,0:T(4,128)S(1)}, u32[]{:S(2)}, u32[]{:S(2)}) collective-permute-start(f32[2,2,22,3,128]{4,3,2,1,0:T(4,128)S(1)} %get-tuple-element.18), channel_id=1, source_target_pairs={{0,8},{8,16},{16,24},{24,32},{32,40},{40,48},{48,56},{1,9},{9,17},... | collective-permute-start | bytes 405512 | tf_op jit(solution)/shard_map/ppermute | solution.py:21
  196.9 8.3 %collective-permute-start.13 = (f32[2,2,3,32,128]{4,3,2,1,0:T(8,128)S(1)}, f32[2,2,3,32,128]{4,3,2,1,0:T(8,128)S(1)}, u32[]{:S(2)}, u32[]{:S(2)}) collective-permute-start(f32[2,2,3,32,128]{4,3,2,1,0:T(8,128)S(1)} %get-tuple-element.25), channel_id=1, source_target_pairs={{64,0},{128,64},{192,128},{65,1},{129,65},{193,129},{66,2},{130,66... | collective-permute-start | bytes 589832 | tf_op jit(solution)/shard_map/ppermute | solution.py:23
  199.2 6.0 %collective-permute-start.12 = (f32[2,2,3,32,128]{4,3,2,1,0:T(8,128)S(1)}, f32[2,2,3,32,128]{4,3,2,1,0:T(8,128)S(1)}, u32[]{:S(2)}, u32[]{:S(2)}) collective-permute-start(f32[2,2,3,32,128]{4,3,2,1,0:T(8,128)S(1)} %get-tuple-element.24), channel_id=1, source_target_pairs={{0,64},{64,128},{128,192},{1,65},{65,129},{129,193},{2,66},{66,130... | collective-permute-start | bytes 589832 | tf_op jit(solution)/shard_map/ppermute | solution.py:21
  205.3 9.8 %collective-permute-start.15 = (f32[2,2,22,3,128]{4,3,2,1,0:T(4,128)S(1)}, f32[2,2,22,3,128]{4,3,2,1,0:T(4,128)S(1)}, u32[]{:S(2)}, u32[]{:S(2)}) collective-permute-start(f32[2,2,22,3,128]{4,3,2,1,0:T(4,128)S(1)} %get-tuple-element.17), channel_id=1, source_target_pairs={{8,0},{16,8},{24,16},{32,24},{40,32},{48,40},{56,48},{9,1},{17,9},... | collective-permute-start | bytes 405512 | tf_op jit(solution)/shard_map/ppermute | solution.py:23
  206.6 13.1 %collective-permute-start.14 = (f32[2,2,22,3,128]{4,3,2,1,0:T(4,128)S(1)}, f32[2,2,22,3,128]{4,3,2,1,0:T(4,128)S(1)}, u32[]{:S(2)}, u32[]{:S(2)}) collective-permute-start(f32[2,2,22,3,128]{4,3,2,1,0:T(4,128)S(1)} %get-tuple-element.16), channel_id=1, source_target_pairs={{0,8},{8,16},{16,24},{24,32},{32,40},{40,48},{48,56},{1,9},{9,17},... | collective-permute-start | bytes 405512 | tf_op jit(solution)/shard_map/ppermute | solution.py:21
  317.1 19.4 %all-to-all-start.2 = ((f32[8,2,8192]{2,1,0:T(2,128)}), f32[8,2,8192]{2,1,0:T(2,128)S(1)}, u32[]{:S(2)}, u32[]{:S(2)}) async-start(f32[8,2,8192]{2,1,0:T(2,128)} %copy.57), calls=%async_computation.2 | async-start | bytes 1048576 | tf_op jit(solution)/shard_map/all_to_all | solution.py:200
  (6 other events, 10.4 us)
where the time goes:
time: 339 us; the launch traced here: 338 us
  blocking collectives  168 us (50%)
  starting transfers between devices  68.8 us (20%)
  other arithmetic  35.5 us (10%)
  waiting for transfers between devices  34.7 us (10%)
  local copies, waits for them, and re-layouts  15.2 us (4%)
  matrix products  10.2 us (3%)
  between operations  5.78 us (2%)
    psum x1, blocking collectives, on_device(): gram_total = lax.psum(gram_part, ('px', 'py', 'dom'))  79.6 us
    psum x1, blocking collectives, on_device(): own_sq = lax.psum(jnp.sum(flat_grad * flat_grad, axis=1), ('px', 'py'))  68.9 us
    ppermute x8, starting transfers between devices, with_halo(): lax.ppermute(tail, axis, [(i, (i + 1) % count) for i in range(ends)])  34.8 us
    all_to_all x1, blocking collectives, on_device(): lax.all_to_all(flat_grad, 'dom', split_axis=1, concat_axis=0, tiled=True)  19.1 us
    ppermute x8, starting transfers between devices, with_halo(): lax.ppermute(head, axis, [((i + 1) % count, i) for i in range(ends)])  17.4 us
    all_to_all x1, waiting for transfers between devices, on_device(): lax.all_to_all(mixed_grad, 'dom', split_axis=0, concat_axis=1, tiled=True)  15.1 us
    mul x9, other arithmetic, axis_term(): flux_face = half_buoy * slope_face  13.4 us
    all_to_all x1, waiting for transfers between devices, on_device(): lax.all_to_all(mixed_model, 'dom', split_axis=0, concat_axis=1, tiled=True)  8.58 us
  transfers between devices with their start and end apart: 19, of which 8 were waited for; matrix products, arithmetic and copies ran while one was open for 10% of the time, Pallas kernels for 0%

commit v1 on v0

--- a/solution.py
+++ b/solution.py
@@ -188,7 +188,7 @@
     gram_part = jnp.dot(
         centered, centered.T, precision=lax.Precision.HIGHEST, preferred_element_type=jnp.float32
     )
-    gram_total = lax.psum(gram_part, ("px", "py", "dom"))
+    gram_total = jnp.sum(lax.all_gather(gram_part, ("px", "py", "dom")), axis=0)
     kernel, row_sum = kernel_from(gram_total, particles)
     mixed_grad = jnp.dot(
         kernel, grad_cols, precision=lax.Precision.HIGHEST, preferred_element_type=jnp.float32

time: 339 us -> 955 us (2.82)
  blocking collectives: 168 us -> 789 us
    all_gather x0 -> x1, blocking collectives: none -> 698 us  [on_device(): gram_total = jnp.sum(lax.all_gather(gram_part, ('px', 'py', 'dom')), axis=0)]
    psum x1 -> x0, blocking collectives: 79.6 us -> none  [on_device(): gram_total = lax.psum(gram_part, ('px', 'py', 'dom'))]
  transfers between devices with their start and end apart: 19 -> 19, of which waited for: 8 -> 8; matrix products, arithmetic and copies ran while one was open for 10% -> 4% of each run, Pallas kernels for 0% -> 0%
where the time goes in v1:
time: 955 us; the launch traced here: 953 us
  blocking collectives  789 us (83%)
  starting transfers between devices  68.7 us (7%)
  other arithmetic  37.4 us (4%)
  waiting for transfers between devices  27.6 us (3%)
  local copies, waits for them, and re-layouts  15.2 us (2%)
  matrix products  10.2 us (1%)
    all_gather x1, blocking collectives, on_device(): gram_total = jnp.sum(lax.all_gather(gram_part, ('px', 'py', 'dom')), axis=0)  698 us
    psum x1, blocking collectives, on_device(): own_sq = lax.psum(jnp.sum(flat_grad * flat_grad, axis=1), ('px', 'py'))  68.5 us
    ppermute x8, starting transfers between devices, with_halo(): lax.ppermute(tail, axis, [(i, (i + 1) % count) for i in range(ends)])  36.7 us
    all_to_all x1, blocking collectives, on_device(): lax.all_to_all(flat_grad, 'dom', split_axis=1, concat_axis=0, tiled=True)  22 us
  transfers between devices with their start and end apart: 19, of which 8 were waited for; matrix products, arithmetic and copies ran while one was open for 4% of the time, Pallas kernels for 0%

profile of v1, /device:TPU:1, one launch (start us, length us, event | category | flops | bytes accessed | tf_op | source)
XLA Modules:
  0.0 953.4 jit_solution(10927374623385748896)
XLA Ops:
  2.5 5.1 collective-permute-start.3
  7.6 1.9 collective-permute-start.2
  9.5 1.9 collective-permute-start
  11.5 2.4 collective-permute-start.1
  15.3 7.7 all-to-all-start
  28.1 3.2 fusion.2
  32.7 5.5 collective-permute-start.4
  42.3 6.9 collective-permute-start.6
  54.2 698.1 %all-gather = f32[4096,16]{1,0:T(8,128)} all-gather(f32[16,16]{1,0:T(8,128)S(1)} %fusion.141), channel_id=2, replica_groups=mesh['px'=4,'py'=8,'dom'=8] {'px','py','dom'}, dimensions={0}, use_global_device_ids=true | all-gather | bytes 263168 | tf_op jit(solution)/shard_map/all_gather | solution.py:191
  758.1 4.3 all-to-all-start.3
  762.5 2.4 fusion.47
  766.2 3.1 fusion.6
  769.3 2.6 fusion.37
  771.9 2.1 all-to-all-done.3
  774.1 2.1 copy.59
  776.2 1.9 all_to_all.59
  778.1 2.4 multiply_subtract_fusion
  780.5 4.3 fusion.84
  785.3 1.9 collective-permute-start.9
  787.2 3.6 collective-permute-start.8
  790.8 2.5 fusion.1
  794.8 5.6 collective-permute-start.10
  802.4 1.9 collective-permute-done.10
  808.5 1.9 collective-permute-start.13
  810.5 4.3 collective-permute-start.12
  814.8 2.5 fusion
  818.7 6.9 collective-permute-start.14
  826.5 4.4 collective-permute-done.14
  837.7 68.5 %psum.7 = f32[2]{0:T(128)S(1)} all-reduce(f32[2]{0:T(128)S(1)} %get-tuple-element.11), channel_id=1, replica_groups=mesh['px'=4,'py'=8,'dom'=8] {'px','py'}, use_global_device_ids=true, to_apply=%region_4.5 | all-reduce | flops 2 | bytes 16 | tf_op jit(solution)/shard_map/psum | solution.py:181
  906.8 22.0 %all_to_all.64 = f32[2,8,8192]{2,0,1:T(2,128)S(1)} all-to-all(f32[2,8,8192]{2,0,1:T(2,128)S(1)} %copy.53), channel_id=1, replica_groups=mesh['px'=4,'py'=8,'dom'=8] {'dom'}, dimensions={1} | all-to-all | bytes 1048576 | tf_op jit(solution)/shard_map/all_to_all | solution.py:185
  930.9 3.5 all-to-all-start.2
  935.2 17.1 %all-to-all-done.2 = f32[8,2,8192]{2,1,0:T(2,128)S(1)} async-done(((f32[8,2,8192]{2,1,0:T(2,128)}), f32[8,2,8192]{2,1,0:T(2,128)S(1)}, u32[]{:S(2)}, u32[]{:S(2)}) %all-to-all-start.2) | async-done | bytes 524320 | tf_op jit(solution)/shard_map/all_to_all | solution.py:200
  (132 shorter events, 43.1 us)
Async XLA Ops:
  0.6 8.9 copy-start.11
  0.6 13.2 %copy-start.8 = (f32[2,16,32,128]{3,2,1,0:T(8,128)S(1)}, f32[2,16,32,128]{3,2,1,0:T(8,128)}, u32[]{:S(2)}) copy-start(f32[2,16,32,128]{3,2,1,0:T(8,128)} %param.11) | copy-start | bytes 1572868
  2.5 37.4 %collective-permute-start.3 = (f32[2,2,3,32,128]{4,3,2,1,0:T(8,128)}, f32[2,2,3,32,128]{4,3,2,1,0:T(8,128)S(1)}, u32[]{:S(2)}, u32[]{:S(2)}) collective-permute-start(f32[2,2,3,32,128]{4,3,2,1,0:T(8,128)} %get-tuple-element.33), channel_id=1, source_target_pairs={{64,0},{128,64},{192,128},{65,1},{129,65},{193,129},{66,2},{130,66... | collective-permute-start | bytes 589832 | tf_op jit(solution)/shard_map/ppermute | solution.py:23
  7.6 32.3 %collective-permute-start.2 = (f32[2,2,3,32,128]{4,3,2,1,0:T(8,128)S(1)}, f32[2,2,3,32,128]{4,3,2,1,0:T(8,128)S(1)}, u32[]{:S(2)}, u32[]{:S(2)}) collective-permute-start(f32[2,2,3,32,128]{4,3,2,1,0:T(8,128)S(1)} %get-tuple-element.32), channel_id=1, source_target_pairs={{0,64},{64,128},{128,192},{1,65},{65,129},{129,193},{2,66},{66,130... | collective-permute-start | bytes 589832 | tf_op jit(solution)/shard_map/ppermute | solution.py:21
  9.5 21.8 %collective-permute-start = (f32[3,32,128]{2,1,0:T(8,128)S(1)}, f32[3,32,128]{2,1,0:T(8,128)S(1)}, u32[]{:S(2)}, u32[]{:S(2)}) collective-permute-start(f32[3,32,128]{2,1,0:T(8,128)S(1)} %get-tuple-element.39), channel_id=1, source_target_pairs={{0,64},{64,128},{128,192},{1,65},{65,129},{129,193},{2,66},{66,130... | collective-permute-start | bytes 147464 | tf_op jit(solution)/shard_map/ppermute | solution.py:21
  11.5 19.9 %collective-permute-start.1 = (f32[3,32,128]{2,1,0:T(8,128)S(1)}, f32[3,32,128]{2,1,0:T(8,128)S(1)}, u32[]{:S(2)}, u32[]{:S(2)}) collective-permute-start(f32[3,32,128]{2,1,0:T(8,128)S(1)} %get-tuple-element.38), channel_id=1, source_target_pairs={{64,0},{128,64},{192,128},{65,1},{129,65},{193,129},{66,2},{130,66... | collective-permute-start | bytes 147464 | tf_op jit(solution)/shard_map/ppermute | solution.py:23
  14.0 8.9 copy-start.16
  14.0 9.2 copy-start.18
  14.0 9.3 copy-start.17
  14.0 9.3 copy-start.14
  14.0 9.3 copy-start.15
  15.3 35.2 %all-to-all-start = ((f32[2,8,8192]{2,0,1:T(2,128)}), f32[2,8,8192]{2,0,1:T(2,128)S(1)}, u32[]{:S(2)}, u32[]{:S(2)}) async-start(f32[2,8,8192]{2,0,1:T(2,128)} %copy.52), calls=%async_computation | async-start | bytes 1048576 | tf_op jit(solution)/shard_map/all_to_all | solution.py:184
  31.4 7.6 collective-permute-start.5
  32.7 6.6 collective-permute-start.4
  39.9 10.6 %copy-start.4 = (f32[2,2,3,32,128]{4,3,2,1,0:T(8,128)}, f32[2,2,3,32,128]{4,3,2,1,0:T(8,128)S(1)}, u32[]{:S(2)}) copy-start(f32[2,2,3,32,128]{4,3,2,1,0:T(8,128)S(1)} %collective-permute-done.3) | copy-start | bytes 589828
  40.2 10.2 %copy-start.6 = (f32[2,2,3,32,128]{4,3,2,1,0:T(8,128)}, f32[2,2,3,32,128]{4,3,2,1,0:T(8,128)S(1)}, u32[]{:S(2)}) copy-start(f32[2,2,3,32,128]{4,3,2,1,0:T(8,128)S(1)} %collective-permute-done.2) | copy-start | bytes 589828
  41.0 723.9 %collective-permute-start.7 = (f32[2,2,22,3,128]{4,3,2,1,0:T(4,128)}, f32[2,2,22,3,128]{4,3,2,1,0:T(4,128)}, u32[]{:S(2)}, u32[]{:S(2)}) collective-permute-start(f32[2,2,22,3,128]{4,3,2,1,0:T(4,128)} %get-tuple-element.21), channel_id=1, source_target_pairs={{8,0},{16,8},{24,16},{32,24},{40,32},{48,40},{56,48},{9,1},{17,9},... | collective-permute-start | bytes 405512 | tf_op jit(solution)/shard_map/ppermute | solution.py:23
  42.3 722.6 %collective-permute-start.6 = (f32[2,2,22,3,128]{4,3,2,1,0:T(4,128)}, f32[2,2,22,3,128]{4,3,2,1,0:T(4,128)}, u32[]{:S(2)}, u32[]{:S(2)}) collective-permute-start(f32[2,2,22,3,128]{4,3,2,1,0:T(4,128)} %get-tuple-element.20), channel_id=1, source_target_pairs={{0,8},{8,16},{16,24},{24,32},{32,40},{40,48},{48,56},{1,9},{9,17},... | collective-permute-start | bytes 405512 | tf_op jit(solution)/shard_map/ppermute | solution.py:21
  758.1 15.9 %all-to-all-start.3 = ((f32[8,2,8192]{2,1,0:T(2,128)}), f32[8,2,8192]{2,1,0:T(2,128)}, u32[]{:S(2)}, u32[]{:S(2)}) async-start(f32[8,2,8192]{2,1,0:T(2,128)} %copy.58), calls=%async_computation.3 | async-start | bytes 1048576 | tf_op jit(solution)/shard_map/all_to_all | solution.py:201
  762.5 2.5 copy-start.5
  762.5 2.5 copy-start.7
  780.5 4.3 copy-start.13
  785.3 8.1 collective-permute-start.9
  787.2 6.2 collective-permute-start.8
  793.5 8.9 collective-permute-start.11
  794.8 5.8 copy-start.3
  794.8 9.5 collective-permute-start.10
  808.5 8.8 collective-permute-start.13
  810.5 6.9 collective-permute-start.12
  817.4 9.1 collective-permute-start.15
  818.7 12.2 %collective-permute-start.14 = (f32[2,2,22,3,128]{4,3,2,1,0:T(4,128)S(1)}, f32[2,2,22,3,128]{4,3,2,1,0:T(4,128)S(1)}, u32[]{:S(2)}, u32[]{:S(2)}) collective-permute-start(f32[2,2,22,3,128]{4,3,2,1,0:T(4,128)S(1)} %get-tuple-element.16), channel_id=1, source_target_pairs={{0,8},{8,16},{16,24},{24,32},{32,40},{40,48},{48,56},{1,9},{9,17},... | collective-permute-start | bytes 405512 | tf_op jit(solution)/shard_map/ppermute | solution.py:21
  930.9 21.4 %all-to-all-start.2 = ((f32[8,2,8192]{2,1,0:T(2,128)}), f32[8,2,8192]{2,1,0:T(2,128)S(1)}, u32[]{:S(2)}, u32[]{:S(2)}) async-start(f32[8,2,8192]{2,1,0:T(2,128)} %copy.55), calls=%async_computation.2 | async-start | bytes 1048576 | tf_op jit(solution)/shard_map/all_to_all | solution.py:200
  (6 other events, 10.4 us)
